TPU v7x, 128 devices: a whole 4x4x4 slice. The times are simulated.
128 devices in a mesh: dom: 32 (over x, z, core), feat: 4 (over y).
Axes of the slice: x: 4, y: 4, z: 4, core: 2. Of those that a mesh axis runs over, the one named last changes fastest.
Arguments:
- features: bfloat16 [32768, 512], P('dom'), may hold values from -96 to 96
- w_query: bfloat16 [512, 512], P(None, 'feat'), may hold values from -0.25 to 0.25
- w_key: bfloat16 [512, 512], P(None, 'feat'), may hold values from -0.25 to 0.25
- w_value: bfloat16 [512, 512], P(None, 'feat'), may hold values from -0.25 to 0.25
- cotangent: bfloat16 [32768, 512], P('dom', 'feat'), may hold values from -6 to 6
- send_rows: int32 [32, 32, 128], P('dom'), may hold values from 0 to 1023, as said below
- halo_count: int32 [32, 32], P(None, 'dom'), may hold values from 0 to 128, as said below
- block_mask: int32 [256, 40], P('dom'), may hold values 0 or 1
- exp_rows: int32 [4, 32768], P(None, 'dom'), may hold values from 0 to 1023, as said below
- global_ids: int32 [128], replicated, may hold values from 0 to 32767, as said below
Outputs:
- attended: bfloat16 [32768, 512], P('dom', 'feat')
- input_grad: bfloat16 [32768, 512], P('dom', 'feat')
Inputs may be any that keep to these rules, and one draw needn't show every extreme that they name: `send_rows`: local row numbers on the sending slab, distinct within each list. `halo_count`: zero from a slab to itself; some receiver gets 128 live slots from every other slab. `exp_rows`: each slab's part of each matching is a permutation of 0 to 1023. `global_ids`: distinct node ids.
All inputs are finite; a program needn't handle non-finite values. No bound on the sum of `block_mask` on one device may be relied on, other than what follows from the above.
Results may differ from a plain program's by a relative error of at most 0.013.
The roundings to bfloat16 on the way count: a program that leaves them out, or rounds other values in their place, can miss the bound.
Values may be sent and summed in bfloat16 or wider, within the bound.
No kernel may reach another device: no remote copies, remote signals or barrier semaphores. Data moves between devices by JAX's collectives and lax.ppermute only.
A program may use at most 128 MiB of HBM per device.

v0:
```python
import math
import jax
import jax.numpy as jnp
from jax import lax
from jax.sharding import PartitionSpec as P

HEAD = 64
BLOCK = 128
EXPANDERS = 4


def swapped_2(value, axis, bit):
    return lax.ppermute(value, axis, [(i, i ^ 1 << bit) for i in range(lax.axis_size(axis))])


def block_allowed(mask_rows, unit, key_live):
    tall = jnp.repeat(mask_rows > 0, unit, axis=0)
    return jnp.repeat(tall, unit, axis=1) & key_live[None, :]


def on_device(
    features,
    w_query,
    w_key,
    w_value,
    cotangent,
    send_rows,
    halo_count,
    block_mask,
    exp_rows,
    global_ids,
):
    node_dev = features.shape[0]
    col_count = w_query.shape[1]
    heads_here = col_count // HEAD
    dom_count = lax.axis_size("dom")
    levels = dom_count.bit_length() - 1
    my_index = lax.axis_index("dom")
    score_scale = 1.0 / math.sqrt(HEAD)
    query = jnp.dot(features, w_query, preferred_element_type=jnp.float32).astype(jnp.bfloat16)
    key_rows = jnp.dot(features, w_key, preferred_element_type=jnp.float32).astype(jnp.bfloat16)
    value_rows = jnp.dot(features, w_value, preferred_element_type=jnp.float32).astype(jnp.bfloat16)
    paired = jnp.concatenate([key_rows, value_rows], axis=1)
    outgoing = paired[send_rows[0]]
    incoming = lax.all_to_all(outgoing, "dom", split_axis=0, concat_axis=0, tiled=True)
    halo_flat = incoming.reshape(dom_count * BLOCK, 2 * col_count)
    slot_live = (jnp.arange(BLOCK, dtype=jnp.int32)[None, :] < halo_count).reshape(-1)
    key_live = jnp.concatenate([jnp.ones((node_dev,), dtype=bool), slot_live])
    cand_key = jnp.concatenate([key_rows, halo_flat[:, :col_count]], axis=0).reshape(
        -1, heads_here, HEAD
    )
    cand_value = jnp.concatenate([value_rows, halo_flat[:, col_count:]], axis=0).reshape(
        -1, heads_here, HEAD
    )
    key_total = cand_key.shape[0]
    partner_list = []
    for matching in range(EXPANDERS):
        swapped = swapped_2(paired, "dom", matching % levels)
        partner_list.append(swapped[exp_rows[matching]])
    partner_pairs = jnp.stack(partner_list)
    is_owner = global_ids // node_dev == my_index
    local_ids = global_ids % node_dev
    picked = jnp.where(is_owner[:, None], paired[local_ids].astype(jnp.float32), 0.0)
    global_pairs = lax.psum(picked.astype(jnp.bfloat16), "dom")
    global_key = global_pairs[:, :col_count].reshape(-1, heads_here, HEAD)
    global_value = global_pairs[:, col_count:].reshape(-1, heads_here, HEAD)
    rows_blk = min(256, node_dev)
    block_count = node_dev // rows_blk
    mask_blk = rows_blk // BLOCK

    def one_block(totals, block_index):
        local_gk, local_gv, global_gk, global_gv = totals
        start = block_index * rows_blk
        query_blk = lax.dynamic_slice_in_dim(query, start, rows_blk, 0).reshape(
            rows_blk, heads_here, HEAD
        )
        grad_blk = lax.dynamic_slice_in_dim(cotangent, start, rows_blk, 0).reshape(
            rows_blk, heads_here, HEAD
        )
        mask_rows = lax.dynamic_slice_in_dim(block_mask, block_index * mask_blk, mask_blk, 0)
        allowed = block_allowed(mask_rows, BLOCK, key_live)
        partner_blk = lax.dynamic_slice_in_dim(partner_pairs, start, rows_blk, 1)
        partner_key = partner_blk[..., :col_count].reshape(EXPANDERS, rows_blk, heads_here, HEAD)
        partner_value = partner_blk[..., col_count:].reshape(EXPANDERS, rows_blk, heads_here, HEAD)
        local_score = (
            jnp.einsum("rhe,khe->rhk", query_blk, cand_key, preferred_element_type=jnp.float32)
            * score_scale
        )
        local_score = jnp.where(allowed[:, None, :], local_score, -jnp.inf)
        partner_score = (
            jnp.einsum("rhe,mrhe->rhm", query_blk, partner_key, preferred_element_type=jnp.float32)
            * score_scale
        )
        global_score = (
            jnp.einsum("rhe,ghe->rhg", query_blk, global_key, preferred_element_type=jnp.float32)
            * score_scale
        )
        top_score = jnp.maximum(
            jnp.maximum(local_score.max(-1), partner_score.max(-1)), global_score.max(-1)
        )[..., None]
        local_exp = jnp.exp(local_score - top_score)
        partner_exp = jnp.exp(partner_score - top_score)
        global_exp = jnp.exp(global_score - top_score)
        denominator = (
            local_exp.sum(-1, keepdims=True)
            + partner_exp.sum(-1, keepdims=True)
            + global_exp.sum(-1, keepdims=True)
        )
        local_prob = local_exp / denominator
        partner_prob = partner_exp / denominator
        global_prob = global_exp / denominator
        local_weight = local_prob.astype(jnp.bfloat16)
        partner_weight = partner_prob.astype(jnp.bfloat16)
        global_weight = global_prob.astype(jnp.bfloat16)
        attended_blk = (
            jnp.einsum("rhk,khe->rhe", local_weight, cand_value, preferred_element_type=jnp.float32)
            + jnp.einsum(
                "rhm,mrhe->rhe", partner_weight, partner_value, preferred_element_type=jnp.float32
            )
            + jnp.einsum(
                "rhg,ghe->rhe", global_weight, global_value, preferred_element_type=jnp.float32
            )
        )
        attended_blk = attended_blk.astype(jnp.bfloat16).reshape(rows_blk, col_count)
        local_dp = jnp.einsum(
            "rhe,khe->rhk", grad_blk, cand_value, preferred_element_type=jnp.float32
        )
        partner_dp = jnp.einsum(
            "rhe,mrhe->rhm", grad_blk, partner_value, preferred_element_type=jnp.float32
        )
        global_dp = jnp.einsum(
            "rhe,ghe->rhg", grad_blk, global_value, preferred_element_type=jnp.float32
        )
        delta = (
            (local_prob * local_dp).sum(-1, keepdims=True)
            + (partner_prob * partner_dp).sum(-1, keepdims=True)
            + (global_prob * global_dp).sum(-1, keepdims=True)
        )
        local_ds = (local_prob * (local_dp - delta) * score_scale).astype(jnp.bfloat16)
        partner_ds = (partner_prob * (partner_dp - delta) * score_scale).astype(jnp.bfloat16)
        global_ds = (global_prob * (global_dp - delta) * score_scale).astype(jnp.bfloat16)
        grad_query_blk = (
            jnp.einsum("rhk,khe->rhe", local_ds, cand_key, preferred_element_type=jnp.float32)
            + jnp.einsum(
                "rhm,mrhe->rhe", partner_ds, partner_key, preferred_element_type=jnp.float32
            )
            + jnp.einsum("rhg,ghe->rhe", global_ds, global_key, preferred_element_type=jnp.float32)
        )
        local_gk = local_gk + jnp.einsum(
            "rhk,rhe->khe", local_ds, query_blk, preferred_element_type=jnp.float32
        )
        local_gv = local_gv + jnp.einsum(
            "rhk,rhe->khe", local_weight, grad_blk, preferred_element_type=jnp.float32
        )
        global_gk = global_gk + jnp.einsum(
            "rhg,rhe->ghe", global_ds, query_blk, preferred_element_type=jnp.float32
        )
        global_gv = global_gv + jnp.einsum(
            "rhg,rhe->ghe", global_weight, grad_blk, preferred_element_type=jnp.float32
        )
        return (
            (local_gk, local_gv, global_gk, global_gv),
            (attended_blk, grad_query_blk.reshape(rows_blk, col_count), partner_ds, partner_weight),
        )

    zero_keys = jnp.zeros((key_total, heads_here, HEAD), jnp.float32)
    zero_globals = jnp.zeros((global_ids.shape[0], heads_here, HEAD), jnp.float32)
    totals, outputs = lax.scan(
        one_block, (zero_keys, zero_keys, zero_globals, zero_globals), jnp.arange(block_count)
    )
    local_gk, local_gv, global_gk, global_gv = totals
    attended_rows, grad_query, partner_ds, partner_weight = outputs
    attended = attended_rows.reshape(node_dev, col_count)
    grad_query = grad_query.reshape(node_dev, col_count)
    partner_ds = partner_ds.reshape(node_dev, heads_here, EXPANDERS)
    partner_weight = partner_weight.reshape(node_dev, heads_here, EXPANDERS)
    key_grads = local_gk.reshape(key_total, col_count)
    value_grads = local_gv.reshape(key_total, col_count)
    pair_grad = jnp.concatenate([key_grads[:node_dev], value_grads[:node_dev]], axis=1)
    halo_back = jnp.concatenate([key_grads[node_dev:], value_grads[node_dev:]], axis=1).reshape(
        dom_count, BLOCK, 2 * col_count
    )
    returned = lax.all_to_all(
        halo_back.astype(jnp.bfloat16), "dom", split_axis=0, concat_axis=0, tiled=True
    )
    pair_grad = pair_grad.at[send_rows[0].reshape(-1)].add(
        returned.reshape(-1, 2 * col_count).astype(jnp.float32)
    )
    for matching in range(EXPANDERS):
        bit_level = matching % levels
        row_order = exp_rows[matching]
        key_term = partner_ds[:, :, matching, None].astype(jnp.float32) * query.reshape(
            node_dev, heads_here, HEAD
        ).astype(jnp.float32)
        value_term = partner_weight[:, :, matching, None].astype(jnp.float32) * cotangent.reshape(
            node_dev, heads_here, HEAD
        ).astype(jnp.float32)
        joined = jnp.concatenate(
            [key_term.reshape(node_dev, col_count), value_term.reshape(node_dev, col_count)], axis=1
        )
        placed = jnp.zeros_like(joined).at[row_order].set(joined)
        pair_grad = pair_grad + swapped_2(placed.astype(jnp.bfloat16), "dom", bit_level).astype(
            placed.dtype
        )
    global_grad = jnp.concatenate(
        [global_gk.reshape(-1, col_count), global_gv.reshape(-1, col_count)], axis=1
    )
    summed = lax.psum(global_grad.astype(jnp.bfloat16), "dom").astype(jnp.float32)
    pair_grad = pair_grad.at[local_ids].add(jnp.where(is_owner[:, None], summed, 0.0))
    feature_terms = (
        jnp.dot(grad_query.astype(jnp.bfloat16), w_query.T, preferred_element_type=jnp.float32)
        + jnp.dot(
            pair_grad[:, :col_count].astype(jnp.bfloat16),
            w_key.T,
            preferred_element_type=jnp.float32,
        )
        + jnp.dot(
            pair_grad[:, col_count:].astype(jnp.bfloat16),
            w_value.T,
            preferred_element_type=jnp.float32,
        )
    )
    input_grad = lax.psum_scatter(feature_terms, "feat", scatter_dimension=1, tiled=True).astype(
        jnp.bfloat16
    )
    return (attended, input_grad)


def solution(mesh):
    return jax.shard_map(
        on_device,
        mesh=mesh,
        in_specs=(
            P("dom", None),
            P(None, "feat"),
            P(None, "feat"),
            P(None, "feat"),
            P("dom", "feat"),
            P("dom", None, None),
            P(None, "dom"),
            P("dom", None),
            P(None, "dom"),
            P(),
        ),
        out_specs=(P("dom", "feat"), P("dom", "feat")),
        check_vma=False,
    )
```

profile of v0, /device:TPU:1, one launch (start us, length us, event | category | flops | bytes accessed | tf_op | source)
XLA Modules:
  0.0 586.4 jit_solution(14606089419128119162)
XLA Ops:
  13.3 3.6 collective-permute-start.2
  19.1 17.0 %gather_fusion = bf16[4096,256]{1,0:T(8,128)(2,1)} fusion(bf16[1024,256]{1,0:T(8,128)(2,1)S(1)} %pad_maximum_fusion.8, s32[4096]{0:T(1024)S(1)} %fusion.59), kind=kCustom, calls=%fused_computation | custom fusion | bytes 4210688 | tf_op jit(solution)/shard_map/gather | solution.py:44
  36.1 5.1 all-to-all-start
  54.5 93.9 %all-reduce.4.cloned.1.call-done = bf16[128,256]{1,0:T(8,128)(2,1)} async-done(((bf16[128,256]{1,0:T(8,128)(2,1)}), bf16[128,256]{1,0:T(8,128)(2,1)}) %all-reduce.4.cloned.1.call-update) | async-done | bytes 65552 | tf_op jit(solution)/shard_map/psum | solution.py:64
  150.6 5.1 gather_fusion.4
  155.7 3.9 gather_fusion.3
  159.6 4.9 gather_fusion.2
  164.6 4.9 gather_fusion.1
  171.0 3.0 fusion.64
  175.5 2.3 copy.178
  177.8 2.2 pad_maximum_fusion.3
  182.1 211.5 %while.25 = (s32[]{:T(128)}, f32[5120,2,64]{0,2,1:T(8,128)}, f32[5120,2,64]{0,2,1:T(8,128)}, f32[128,2,64]{0,2,1:T(8,128)}, f32[128,2,64]{0,2,1:T(8,128)}, /*ind...) while((s32[]{:T(128)}, f32[5120,2,64]{0,2,1:T(8,128)}, ...), condition=%wide.region_11.12_spmd.clone, body=%wide.region_1.11_spmd.clone.sunk | while | flops 2151969280 | bytes 260182544 | solution.py:168
  190.4 3.6 bitcast_reduce_fusion.2
  194.1 3.0 fusion.164
  198.0 4.2 fusion.173
  203.6 8.3 %fusion.169 = f32[5120,2,64]{0,2,1:T(8,128)} fusion(bf16[256,2,64]{0,2,1:T(8,128)(2,1)S(1)} %bitcast.353, f32[5120,2,64]{0,2,1:T(8,128)} %get-tuple-element.548, pred[]{:T(512)S(6)} %compare.7, f32[2,256,5120]{2,1,0:T(8,128)} %copy-done.2, f32[256,2]{0,1:T(2,128)S(1)} %add_add_fusion.5, f32[256,2]{0,1:T(2,128)S(1)} %maximum_maximum_fusion.2, ...), kind=kOutput, calls=%fused_computation.25.clone.1 | convolution fusion | flops 349962240 | bytes 17108992 | tf_op jit(solution)/shard_map/while/body/eval_jaxpr/rhk,rhe->khe/dot_general | solution.py:152
  212.0 7.3 %fusion.166 = (f32[256,2]{0,1:T(2,128)S(1)}, f32[2,256,5120]{2,1,0:T(8,128)}) fusion(f32[256,2]{0,1:T(2,128)S(1)} %add_add_fusion.5, f32[256,2]{0,1:T(2,128)S(1)} %maximum_maximum_fusion.2, f32[2,256,5120]{2,1,0:T(8,128)S(1)} %bitcast.324, pred[256,5120]{1,0:T(8,128)(4,1)S(1)} %bitcast_and_fusion.2, bf16[256,2,64]{0,2,1:T(8,128)(2,1)S(1)} %bitcast.354, ...), kind=kOutput, calls=%fused_computation.14.clone.1 | convolution fusion | flops 351272448 | bytes 23664640 | tf_op jit(solution)/shard_map/while/body/eval_jaxpr/rhe,khe->rhk/dot_general | solution.py:125
  219.4 7.1 %fusion.167 = bf16[256,2,5120]{2,0,1:T(8,128)(2,1)S(1)} fusion(f32[2,256,5120]{2,1,0:T(8,128)} %get-tuple-element.506, f32[256,2]{0,1:T(2,128)S(1)} %add_add_fusion.6, f32[256,2]{0,1:T(2,128)S(1)} %add_add_fusion.5, f32[256,2]{0,1:T(2,128)S(1)} %maximum_maximum_fusion.2, f32[2,256,5120]{2,1,0:T(8,128)S(1)} %bitcast.324, ...), kind=kLoop, calls=%fused_computation.17.clone.1 | loop fusion | flops 20971520 | bytes 27531264 | tf_op jit(solution)/shard_map/while/body/eval_jaxpr/convert_element_type | solution.py:139
  241.8 3.6 bitcast_reduce_fusion.2
  245.5 3.0 fusion.164
  249.5 4.2 fusion.173
  256.0 9.1 %fusion.169 = f32[5120,2,64]{0,2,1:T(8,128)} fusion(bf16[256,2,64]{0,2,1:T(8,128)(2,1)S(1)} %bitcast.353, f32[5120,2,64]{0,2,1:T(8,128)} %get-tuple-element.548, pred[]{:T(512)S(6)} %compare.7, f32[2,256,5120]{2,1,0:T(8,128)} %copy-done.2, f32[256,2]{0,1:T(2,128)S(1)} %add_add_fusion.5, f32[256,2]{0,1:T(2,128)S(1)} %maximum_maximum_fusion.2, ...), kind=kOutput, calls=%fused_computation.25.clone.1 | convolution fusion | flops 349962240 | bytes 17108992 | tf_op jit(solution)/shard_map/while/body/eval_jaxpr/rhk,rhe->khe/dot_general | solution.py:152
  265.1 7.3 %fusion.166 = (f32[256,2]{0,1:T(2,128)S(1)}, f32[2,256,5120]{2,1,0:T(8,128)}) fusion(f32[256,2]{0,1:T(2,128)S(1)} %add_add_fusion.5, f32[256,2]{0,1:T(2,128)S(1)} %maximum_maximum_fusion.2, f32[2,256,5120]{2,1,0:T(8,128)S(1)} %bitcast.324, pred[256,5120]{1,0:T(8,128)(4,1)S(1)} %bitcast_and_fusion.2, bf16[256,2,64]{0,2,1:T(8,128)(2,1)S(1)} %bitcast.354, ...), kind=kOutput, calls=%fused_computation.14.clone.1 | convolution fusion | flops 351272448 | bytes 23664640 | tf_op jit(solution)/shard_map/while/body/eval_jaxpr/rhe,khe->rhk/dot_general | solution.py:125
  272.6 7.1 %fusion.167 = bf16[256,2,5120]{2,0,1:T(8,128)(2,1)S(1)} fusion(f32[2,256,5120]{2,1,0:T(8,128)} %get-tuple-element.506, f32[256,2]{0,1:T(2,128)S(1)} %add_add_fusion.6, f32[256,2]{0,1:T(2,128)S(1)} %add_add_fusion.5, f32[256,2]{0,1:T(2,128)S(1)} %maximum_maximum_fusion.2, f32[2,256,5120]{2,1,0:T(8,128)S(1)} %bitcast.324, ...), kind=kLoop, calls=%fused_computation.17.clone.1 | loop fusion | flops 20971520 | bytes 27531264 | tf_op jit(solution)/shard_map/while/body/eval_jaxpr/convert_element_type | solution.py:139
  295.0 3.6 bitcast_reduce_fusion.2
  298.7 3.0 fusion.164
  302.8 4.2 fusion.173
  309.2 9.1 %fusion.169 = f32[5120,2,64]{0,2,1:T(8,128)} fusion(bf16[256,2,64]{0,2,1:T(8,128)(2,1)S(1)} %bitcast.353, f32[5120,2,64]{0,2,1:T(8,128)} %get-tuple-element.548, pred[]{:T(512)S(6)} %compare.7, f32[2,256,5120]{2,1,0:T(8,128)} %copy-done.2, f32[256,2]{0,1:T(2,128)S(1)} %add_add_fusion.5, f32[256,2]{0,1:T(2,128)S(1)} %maximum_maximum_fusion.2, ...), kind=kOutput, calls=%fused_computation.25.clone.1 | convolution fusion | flops 349962240 | bytes 17108992 | tf_op jit(solution)/shard_map/while/body/eval_jaxpr/rhk,rhe->khe/dot_general | solution.py:152
  318.4 7.3 %fusion.166 = (f32[256,2]{0,1:T(2,128)S(1)}, f32[2,256,5120]{2,1,0:T(8,128)}) fusion(f32[256,2]{0,1:T(2,128)S(1)} %add_add_fusion.5, f32[256,2]{0,1:T(2,128)S(1)} %maximum_maximum_fusion.2, f32[2,256,5120]{2,1,0:T(8,128)S(1)} %bitcast.324, pred[256,5120]{1,0:T(8,128)(4,1)S(1)} %bitcast_and_fusion.2, bf16[256,2,64]{0,2,1:T(8,128)(2,1)S(1)} %bitcast.354, ...), kind=kOutput, calls=%fused_computation.14.clone.1 | convolution fusion | flops 351272448 | bytes 23664640 | tf_op jit(solution)/shard_map/while/body/eval_jaxpr/rhe,khe->rhk/dot_general | solution.py:125
  325.8 7.1 %fusion.167 = bf16[256,2,5120]{2,0,1:T(8,128)(2,1)S(1)} fusion(f32[2,256,5120]{2,1,0:T(8,128)} %get-tuple-element.506, f32[256,2]{0,1:T(2,128)S(1)} %add_add_fusion.6, f32[256,2]{0,1:T(2,128)S(1)} %add_add_fusion.5, f32[256,2]{0,1:T(2,128)S(1)} %maximum_maximum_fusion.2, f32[2,256,5120]{2,1,0:T(8,128)S(1)} %bitcast.324, ...), kind=kLoop, calls=%fused_computation.17.clone.1 | loop fusion | flops 20971520 | bytes 27531264 | tf_op jit(solution)/shard_map/while/body/eval_jaxpr/convert_element_type | solution.py:139
  348.2 3.6 bitcast_reduce_fusion.2
  351.9 3.0 fusion.164
  355.8 4.2 fusion.173
  362.3 9.1 %fusion.169 = f32[5120,2,64]{0,2,1:T(8,128)} fusion(bf16[256,2,64]{0,2,1:T(8,128)(2,1)S(1)} %bitcast.353, f32[5120,2,64]{0,2,1:T(8,128)} %get-tuple-element.548, pred[]{:T(512)S(6)} %compare.7, f32[2,256,5120]{2,1,0:T(8,128)} %copy-done.2, f32[256,2]{0,1:T(2,128)S(1)} %add_add_fusion.5, f32[256,2]{0,1:T(2,128)S(1)} %maximum_maximum_fusion.2, ...), kind=kOutput, calls=%fused_computation.25.clone.1 | convolution fusion | flops 349962240 | bytes 17108992 | tf_op jit(solution)/shard_map/while/body/eval_jaxpr/rhk,rhe->khe/dot_general | solution.py:152
  371.5 7.3 %fusion.166 = (f32[256,2]{0,1:T(2,128)S(1)}, f32[2,256,5120]{2,1,0:T(8,128)}) fusion(f32[256,2]{0,1:T(2,128)S(1)} %add_add_fusion.5, f32[256,2]{0,1:T(2,128)S(1)} %maximum_maximum_fusion.2, f32[2,256,5120]{2,1,0:T(8,128)S(1)} %bitcast.324, pred[256,5120]{1,0:T(8,128)(4,1)S(1)} %bitcast_and_fusion.2, bf16[256,2,64]{0,2,1:T(8,128)(2,1)S(1)} %bitcast.354, ...), kind=kOutput, calls=%fused_computation.14.clone.1 | convolution fusion | flops 351272448 | bytes 23664640 | tf_op jit(solution)/shard_map/while/body/eval_jaxpr/rhe,khe->rhk/dot_general | solution.py:125
  378.9 7.1 %fusion.167 = bf16[256,2,5120]{2,0,1:T(8,128)(2,1)S(1)} fusion(f32[2,256,5120]{2,1,0:T(8,128)} %get-tuple-element.506, f32[256,2]{0,1:T(2,128)S(1)} %add_add_fusion.6, f32[256,2]{0,1:T(2,128)S(1)} %add_add_fusion.5, f32[256,2]{0,1:T(2,128)S(1)} %maximum_maximum_fusion.2, f32[2,256,5120]{2,1,0:T(8,128)S(1)} %bitcast.324, ...), kind=kLoop, calls=%fused_computation.17.clone.1 | loop fusion | flops 20971520 | bytes 27531264 | tf_op jit(solution)/shard_map/while/body/eval_jaxpr/convert_element_type | solution.py:139
  401.4 5.0 all-to-all-start.1
  410.4 5.5 scatter_custom_fusion
  419.3 5.5 scatter_custom_fusion.1
  427.1 5.5 scatter_custom_fusion.2
  433.9 5.4 scatter_custom_fusion.3
  441.6 2.7 collective-permute-start.6
  453.7 2.5 collective-permute-done.6
  456.2 11.4 %collective-permute-done.5 = bf16[1024,256]{1,0:T(8,128)(2,1)} collective-permute-done((bf16[1024,256]{1,0:T(8,128)(2,1)}, bf16[1024,256]{1,0:T(8,128)(2,1)}, u32[]{:S(2)}, u32[]{:S(2)}) %collective-permute-start.5) | collective-permute-done | bytes 524320 | tf_op jit(solution)/shard_map/ppermute | solution.py:13
  469.4 4.1 copy.128
  473.5 23.4 %scatter_custom_fusion.4 = f32[1024,256]{1,0:T(8,128)S(1)} fusion(f32[1024,256]{1,0:T(8,128)S(1)} %fusion.41, s32[4096]{0:T(1024)S(1)} %bitcast.365, bf16[4096,256]{1,0:T(8,128)(2,1)} %bitcast.333), kind=kCustom, calls=%fused_computation.82 | custom fusion | flops 2097152 | bytes 3145728 | tf_op jit(solution)/shard_map/scatter-add | solution.py:186
  497.0 48.0 %all-reduce.6.cloned.1.call-done = bf16[128,256]{1,0:T(8,128)(2,1)} async-done(((bf16[128,256]{1,0:T(8,128)(2,1)}), bf16[128,256]{1,0:T(8,128)(2,1)}) %all-reduce.6.cloned.1.call-update) | async-done | bytes 65552 | tf_op jit(solution)/shard_map/psum | solution.py:208
  549.5 28.4 %reduce-scatter.2.cloned.1.call-done = f32[1024,128]{1,0:T(8,128)} async-done(((f32[1024,512]{1,0:T(8,128)}), f32[1024,128]{1,0:T(8,128)}) %reduce-scatter.2.cloned.1.call-update) | async-done | bytes 524304 | tf_op jit(solution)/shard_map/reduce_scatter | solution.py:223
  (444 shorter events, 134.9 us)
Async XLA Ops:
  7.2 11.9 %copy-start.27 = (s32[1,32,128]{2,1,0:T(8,128)S(1)}, s32[1,32,128]{2,1,0:T(8,128)}, u32[]{:S(2)}) copy-start(s32[1,32,128]{2,1,0:T(8,128)} %param.17) | copy-start | bytes 49156
  11.2 139.4 %collective-permute-start.3 = (bf16[1024,256]{1,0:T(8,128)(2,1)S(1)}, bf16[1024,256]{1,0:T(8,128)(2,1)}, u32[]{:S(2)}, u32[]{:S(2)}) collective-permute-start(bf16[1024,256]{1,0:T(8,128)(2,1)S(1)} %pad_maximum_fusion.8), channel_id=1, source_target_pairs={{0,32},{4,36},{8,40},{12,44},{16,48},{20,52},{24,56},{28,60},{32,0... | collective-permute-start | bytes 1572872 | tf_op jit(solution)/shard_map/ppermute | solution.py:13
  13.3 142.4 %collective-permute-start.2 = (bf16[1024,256]{1,0:T(8,128)(2,1)S(1)}, bf16[1024,256]{1,0:T(8,128)(2,1)S(1)}, u32[]{:S(2)}, u32[]{:S(2)}) collective-permute-start(bf16[1024,256]{1,0:T(8,128)(2,1)S(1)} %pad_maximum_fusion.8), channel_id=1, source_target_pairs={{0,16},{4,20},{8,24},{12,28},{16,0},{20,4},{24,8},{28,12},{32,48},... | collective-permute-start | bytes 1572872 | tf_op jit(solution)/shard_map/ppermute | solution.py:13
  16.9 142.8 %collective-permute-start.1 = (bf16[1024,256]{1,0:T(8,128)(2,1)S(1)}, bf16[1024,256]{1,0:T(8,128)(2,1)S(1)}, u32[]{:S(2)}, u32[]{:S(2)}) collective-permute-start(bf16[1024,256]{1,0:T(8,128)(2,1)S(1)} %pad_maximum_fusion.8), channel_id=1, source_target_pairs={{0,8},{4,12},{8,0},{12,4},{16,24},{20,28},{24,16},{28,20},{32,40},... | collective-permute-start | bytes 1572872 | tf_op jit(solution)/shard_map/ppermute | solution.py:13
  17.6 147.0 %collective-permute-start = (bf16[1024,256]{1,0:T(8,128)(2,1)S(1)}, bf16[1024,256]{1,0:T(8,128)(2,1)S(1)}, u32[]{:S(2)}, u32[]{:S(2)}) collective-permute-start(bf16[1024,256]{1,0:T(8,128)(2,1)S(1)} %pad_maximum_fusion.8), channel_id=1, source_target_pairs={{0,4},{4,0},{8,12},{12,8},{16,20},{20,16},{24,28},{28,24},{32,36},... | collective-permute-start | bytes 1572872 | tf_op jit(solution)/shard_map/ppermute | solution.py:13
  36.1 10.7 %copy-start.30 = (s32[4,1024]{1,0:T(4,128)S(1)}, s32[4,1024]{1,0:T(4,128)}, u32[]{:S(2)}) copy-start(s32[4,1024]{1,0:T(4,128)} %param.20) | copy-start | bytes 49156
  36.1 12.0 %copy-start.22 = (bf16[512,128]{1,0:T(8,128)(2,1)S(1)}, bf16[512,128]{1,0:T(8,128)(2,1)}, u32[]{:S(2)}) copy-start(bf16[512,128]{1,0:T(8,128)(2,1)} %param.13) | copy-start | bytes 393220
  36.1 134.9 %all-to-all-start = ((bf16[32,128,256]{2,1,0:T(8,128)(2,1)}), bf16[32,128,256]{2,1,0:T(8,128)(2,1)}, u32[]{:S(2)}, u32[]{:S(2)}) async-start(bf16[32,128,256]{2,1,0:T(8,128)(2,1)} %bitcast.334), calls=%async_computation | async-start | bytes 4194304 | tf_op jit(solution)/shard_map/all_to_all | solution.py:45
  41.2 107.2 %all-reduce.4.cloned.1.call-start = ((), (), s32[]{:S(2)}) async-start(), calls=%async_computation.3 | async-start | bytes 131072 | tf_op jit(solution)/shard_map/psum | solution.py:64
  203.4 8.6 %slice-start = ((s8[10485760]{0:T(1024)(128)(4,1)}), s8[4194304]{0:T(1024)(128)(4,1)S(1)}, s32[]{:S(2)}) async-start(s8[10485760]{0:T(1024)(128)(4,1)} %bitcast.323), calls=%async_computation.6 | async-start | bytes 8388608 | tf_op jit(solution)/shard_map/while
  203.6 8.4 %slice-start.1 = ((s8[10485760]{0:T(1024)(128)(4,1)}), s8[4194304]{0:T(1024)(128)(4,1)S(1)}, s32[]{:S(2)}) async-start(s8[10485760]{0:T(1024)(128)(4,1)} %bitcast.323), calls=%async_computation.7 | async-start | bytes 8388608 | tf_op jit(solution)/shard_map/while
  203.6 8.4 %slice-start.2 = ((s8[10485760]{0:T(1024)(128)(4,1)}), s8[2097152]{0:T(1024)(128)(4,1)S(1)}, s32[]{:S(2)}) async-start(s8[10485760]{0:T(1024)(128)(4,1)} %bitcast.323), calls=%async_computation.8 | async-start | bytes 4194304 | tf_op jit(solution)/shard_map/while
  203.6 8.3 %copy-start.21 = (bf16[5120,2,64]{0,2,1:T(8,128)(2,1)S(1)}, bf16[5120,2,64]{0,2,1:T(8,128)(2,1)}, u32[]{:S(2)}) copy-start(bf16[5120,2,64]{0,2,1:T(8,128)(2,1)} %get-tuple-element.589) | copy-start | bytes 3932164 | tf_op jit(solution)/shard_map/while
  219.4 7.8 %copy-start.13 = (f32[128,2,64]{0,2,1:T(8,128)S(1)}, f32[128,2,64]{0,2,1:T(8,128)}, u32[]{:S(2)}) copy-start(f32[128,2,64]{0,2,1:T(8,128)} %get-tuple-element.549) | copy-start | bytes 196612 | tf_op jit(solution)/shard_map/while
  219.4 8.9 %copy-start.5 = (bf16[5120,2,64]{0,2,1:T(8,128)(2,1)S(1)}, bf16[5120,2,64]{0,2,1:T(8,128)(2,1)}, u32[]{:S(2)}) copy-start(bf16[5120,2,64]{0,2,1:T(8,128)(2,1)} %get-tuple-element.585) | copy-start | bytes 3932164 | tf_op jit(solution)/shard_map/while
  255.7 9.4 %slice-start = ((s8[10485760]{0:T(1024)(128)(4,1)}), s8[4194304]{0:T(1024)(128)(4,1)S(1)}, s32[]{:S(2)}) async-start(s8[10485760]{0:T(1024)(128)(4,1)} %bitcast.323), calls=%async_computation.6 | async-start | bytes 8388608 | tf_op jit(solution)/shard_map/while
  256.0 9.2 %slice-start.1 = ((s8[10485760]{0:T(1024)(128)(4,1)}), s8[4194304]{0:T(1024)(128)(4,1)S(1)}, s32[]{:S(2)}) async-start(s8[10485760]{0:T(1024)(128)(4,1)} %bitcast.323), calls=%async_computation.7 | async-start | bytes 8388608 | tf_op jit(solution)/shard_map/while
  256.0 9.2 %slice-start.2 = ((s8[10485760]{0:T(1024)(128)(4,1)}), s8[2097152]{0:T(1024)(128)(4,1)S(1)}, s32[]{:S(2)}) async-start(s8[10485760]{0:T(1024)(128)(4,1)} %bitcast.323), calls=%async_computation.8 | async-start | bytes 4194304 | tf_op jit(solution)/shard_map/while
  256.0 9.2 %copy-start.21 = (bf16[5120,2,64]{0,2,1:T(8,128)(2,1)S(1)}, bf16[5120,2,64]{0,2,1:T(8,128)(2,1)}, u32[]{:S(2)}) copy-start(bf16[5120,2,64]{0,2,1:T(8,128)(2,1)} %get-tuple-element.589) | copy-start | bytes 3932164 | tf_op jit(solution)/shard_map/while
  272.6 7.8 %copy-start.13 = (f32[128,2,64]{0,2,1:T(8,128)S(1)}, f32[128,2,64]{0,2,1:T(8,128)}, u32[]{:S(2)}) copy-start(f32[128,2,64]{0,2,1:T(8,128)} %get-tuple-element.549) | copy-start | bytes 196612 | tf_op jit(solution)/shard_map/while
  272.6 8.9 %copy-start.5 = (bf16[5120,2,64]{0,2,1:T(8,128)(2,1)S(1)}, bf16[5120,2,64]{0,2,1:T(8,128)(2,1)}, u32[]{:S(2)}) copy-start(bf16[5120,2,64]{0,2,1:T(8,128)(2,1)} %get-tuple-element.585) | copy-start | bytes 3932164 | tf_op jit(solution)/shard_map/while
  308.9 9.4 %slice-start = ((s8[10485760]{0:T(1024)(128)(4,1)}), s8[4194304]{0:T(1024)(128)(4,1)S(1)}, s32[]{:S(2)}) async-start(s8[10485760]{0:T(1024)(128)(4,1)} %bitcast.323), calls=%async_computation.6 | async-start | bytes 8388608 | tf_op jit(solution)/shard_map/while
  309.2 9.2 %slice-start.1 = ((s8[10485760]{0:T(1024)(128)(4,1)}), s8[4194304]{0:T(1024)(128)(4,1)S(1)}, s32[]{:S(2)}) async-start(s8[10485760]{0:T(1024)(128)(4,1)} %bitcast.323), calls=%async_computation.7 | async-start | bytes 8388608 | tf_op jit(solution)/shard_map/while
  309.2 9.2 %slice-start.2 = ((s8[10485760]{0:T(1024)(128)(4,1)}), s8[2097152]{0:T(1024)(128)(4,1)S(1)}, s32[]{:S(2)}) async-start(s8[10485760]{0:T(1024)(128)(4,1)} %bitcast.323), calls=%async_computation.8 | async-start | bytes 4194304 | tf_op jit(solution)/shard_map/while
  309.2 9.2 %copy-start.21 = (bf16[5120,2,64]{0,2,1:T(8,128)(2,1)S(1)}, bf16[5120,2,64]{0,2,1:T(8,128)(2,1)}, u32[]{:S(2)}) copy-start(bf16[5120,2,64]{0,2,1:T(8,128)(2,1)} %get-tuple-element.589) | copy-start | bytes 3932164 | tf_op jit(solution)/shard_map/while
  325.8 8.9 %copy-start.5 = (bf16[5120,2,64]{0,2,1:T(8,128)(2,1)S(1)}, bf16[5120,2,64]{0,2,1:T(8,128)(2,1)}, u32[]{:S(2)}) copy-start(bf16[5120,2,64]{0,2,1:T(8,128)(2,1)} %get-tuple-element.585) | copy-start | bytes 3932164 | tf_op jit(solution)/shard_map/while
  362.0 9.4 %slice-start = ((s8[10485760]{0:T(1024)(128)(4,1)}), s8[4194304]{0:T(1024)(128)(4,1)S(1)}, s32[]{:S(2)}) async-start(s8[10485760]{0:T(1024)(128)(4,1)} %bitcast.323), calls=%async_computation.6 | async-start | bytes 8388608 | tf_op jit(solution)/shard_map/while
  362.3 9.2 %slice-start.1 = ((s8[10485760]{0:T(1024)(128)(4,1)}), s8[4194304]{0:T(1024)(128)(4,1)S(1)}, s32[]{:S(2)}) async-start(s8[10485760]{0:T(1024)(128)(4,1)} %bitcast.323), calls=%async_computation.7 | async-start | bytes 8388608 | tf_op jit(solution)/shard_map/while
  362.3 9.2 %slice-start.2 = ((s8[10485760]{0:T(1024)(128)(4,1)}), s8[2097152]{0:T(1024)(128)(4,1)S(1)}, s32[]{:S(2)}) async-start(s8[10485760]{0:T(1024)(128)(4,1)} %bitcast.323), calls=%async_computation.8 | async-start | bytes 4194304 | tf_op jit(solution)/shard_map/while
  362.3 9.2 %copy-start.21 = (bf16[5120,2,64]{0,2,1:T(8,128)(2,1)S(1)}, bf16[5120,2,64]{0,2,1:T(8,128)(2,1)}, u32[]{:S(2)}) copy-start(bf16[5120,2,64]{0,2,1:T(8,128)(2,1)} %get-tuple-element.589) | copy-start | bytes 3932164 | tf_op jit(solution)/shard_map/while
  378.9 8.9 %copy-start.5 = (bf16[5120,2,64]{0,2,1:T(8,128)(2,1)S(1)}, bf16[5120,2,64]{0,2,1:T(8,128)(2,1)}, u32[]{:S(2)}) copy-start(bf16[5120,2,64]{0,2,1:T(8,128)(2,1)} %get-tuple-element.585) | copy-start | bytes 3932164 | tf_op jit(solution)/shard_map/while
  401.4 68.1 %all-to-all-start.1 = ((bf16[32,128,256]{1,2,0:T(8,128)(2,1)}), bf16[32,128,256]{1,2,0:T(8,128)(2,1)}, u32[]{:S(2)}, u32[]{:S(2)}) async-start(bf16[32,128,256]{1,2,0:T(8,128)(2,1)} %copy.127), calls=%async_computation.1 | async-start | bytes 4194304 | tf_op jit(solution)/shard_map/all_to_all | solution.py:183
  406.4 138.6 %all-reduce.6.cloned.1.call-start = ((), (), s32[]{:S(2)}) async-start(), calls=%async_computation.4 | async-start | bytes 131072 | tf_op jit(solution)/shard_map/psum | solution.py:208
  433.5 12.2 %copy-start.28 = (s32[1,32,128]{2,1,0:T(8,128)S(1)}, s32[1,32,128]{2,1,0:T(8,128)}, u32[]{:S(2)}) copy-start(s32[1,32,128]{2,1,0:T(8,128)} %param.17) | copy-start | bytes 49156
  433.9 14.1 %copy-start.15 = (f32[128,2,64]{0,2,1:T(8,128)S(1)}, f32[128,2,64]{0,2,1:T(8,128)}, u32[]{:S(2)}) copy-start(f32[128,2,64]{0,2,1:T(8,128)} %get-tuple-element.642) | copy-start | bytes 196612
  440.2 11.7 %copy-start.23 = (bf16[512,128]{1,0:T(8,128)(2,1)S(1)}, bf16[512,128]{1,0:T(8,128)(2,1)}, u32[]{:S(2)}) copy-start(bf16[512,128]{1,0:T(8,128)(2,1)} %param.13) | copy-start | bytes 393220
  440.2 11.7 %copy-start.26 = (bf16[4,256,128]{2,1,0:T(8,128)(2,1)S(1)}, bf16[4,256,128]{2,1,0:T(8,128)(2,1)}, u32[]{:S(2)}) copy-start(bf16[4,256,128]{2,1,0:T(8,128)(2,1)} %get-tuple-element.645) | copy-start | bytes 786436
  440.2 13.5 %collective-permute-start.7 = (bf16[1024,256]{1,0:T(8,128)(2,1)}, bf16[1024,256]{1,0:T(8,128)(2,1)}, u32[]{:S(2)}, u32[]{:S(2)}) collective-permute-start(bf16[1024,256]{1,0:T(8,128)(2,1)} %convert_element_type.125), channel_id=1, source_target_pairs={{0,32},{4,36},{8,40},{12,44},{16,48},{20,52},{24,56},{28,60},{32,0... | collective-permute-start | bytes 1572872 | tf_op jit(solution)/shard_map/ppermute | solution.py:13
  441.6 14.7 %collective-permute-start.6 = (bf16[1024,256]{1,0:T(8,128)(2,1)}, bf16[1024,256]{1,0:T(8,128)(2,1)}, u32[]{:S(2)}, u32[]{:S(2)}) collective-permute-start(bf16[1024,256]{1,0:T(8,128)(2,1)} %convert_element_type.123), channel_id=1, source_target_pairs={{0,16},{4,20},{8,24},{12,28},{16,0},{20,4},{24,8},{28,12},{32,48},... | collective-permute-start | bytes 1572872 | tf_op jit(solution)/shard_map/ppermute | solution.py:13
  444.3 23.3 %collective-permute-start.5 = (bf16[1024,256]{1,0:T(8,128)(2,1)}, bf16[1024,256]{1,0:T(8,128)(2,1)}, u32[]{:S(2)}, u32[]{:S(2)}) collective-permute-start(bf16[1024,256]{1,0:T(8,128)(2,1)} %convert_element_type.121), channel_id=1, source_target_pairs={{0,8},{4,12},{8,0},{12,4},{16,24},{20,28},{24,16},{28,20},{32,40},... | collective-permute-start | bytes 1572872 | tf_op jit(solution)/shard_map/ppermute | solution.py:13
  444.6 23.0 %collective-permute-start.4 = (bf16[1024,256]{1,0:T(8,128)(2,1)}, bf16[1024,256]{1,0:T(8,128)(2,1)}, u32[]{:S(2)}, u32[]{:S(2)}) collective-permute-start(bf16[1024,256]{1,0:T(8,128)(2,1)} %convert_element_type.119), channel_id=1, source_target_pairs={{0,4},{4,0},{8,12},{12,8},{16,20},{20,16},{24,28},{28,24},{32,36},... | collective-permute-start | bytes 1572872 | tf_op jit(solution)/shard_map/ppermute | solution.py:13
  449.7 128.2 %reduce-scatter.2.cloned.1.call-start = ((), (), s32[]{:S(2)}) async-start(), calls=%async_computation.5 | async-start | bytes 2621440 | tf_op jit(solution)/shard_map/reduce_scatter | solution.py:223
  451.9 15.7 %copy-start.18 = (f32[1024,128]{1,0:T(8,128)S(1)}, f32[1024,128]{1,0:T(8,128)}, u32[]{:S(2)}) copy-start(f32[1024,128]{1,0:T(8,128)} %copy.118) | copy-start | bytes 1572868
  451.9 15.7 %copy-start.19 = (f32[1024,128]{1,0:T(8,128)S(1)}, f32[1024,128]{1,0:T(8,128)}, u32[]{:S(2)}) copy-start(f32[1024,128]{1,0:T(8,128)} %copy.119) | copy-start | bytes 1572868
  473.5 71.5 %copy-start.35 = (pred[128]{0:T(512)(128)(4,1)S(1)}, pred[128]{0:T(512)(128)(4,1)}, u32[]{:S(2)}) copy-start(pred[128]{0:T(512)(128)(4,1)} %fusion.61) | copy-start | bytes 388
  473.5 73.6 %copy-start.24 = (bf16[512,128]{1,0:T(8,128)(2,1)S(1)}, bf16[512,128]{1,0:T(8,128)(2,1)}, u32[]{:S(2)}) copy-start(bf16[512,128]{1,0:T(8,128)(2,1)} %param.14) | copy-start | bytes 393220
  497.0 50.6 %copy-start.25 = (bf16[512,128]{1,0:T(8,128)(2,1)S(1)}, bf16[512,128]{1,0:T(8,128)(2,1)}, u32[]{:S(2)}) copy-start(bf16[512,128]{1,0:T(8,128)(2,1)} %param.15) | copy-start | bytes 393220
  547.6 32.1 %copy-start.1 = (bf16[1024,512]{1,0:T(8,128)(2,1)S(1)}, bf16[1024,512]{1,0:T(8,128)(2,1)}, u32[]{:S(2)}) copy-start(bf16[1024,512]{1,0:T(8,128)(2,1)} %param.12) | copy-start | bytes 3145732
  (61 other events, 219.4 us)
Sparse Core Ops, SparseCore 0:
  46.9 101.4 all-reduce.3
  449.9 95.0 all-reduce.5
  549.6 28.2 reduce-scatter.1
where the time goes:
time: 594 us; the launch traced here: 586 us
  waiting for transfers between devices  186 us (31%)
  matrix products  128 us (22%)
  local copies, waits for them, and re-layouts  118 us (20%)
  other arithmetic  109 us (18%)
  starting transfers between devices  23.7 us (4%)
  between operations  14.5 us (2%)
  loops' own time  7.29 us (1%)
    psum x1, waiting for transfers between devices, on_device(): global_pairs = lax.psum(picked.astype(jnp.bfloat16), 'dom')  93.9 us
    psum x1, waiting for transfers between devices, on_device(): lax.psum(global_grad.astype(jnp.bfloat16), 'dom').astype(jnp.float32)  48 us
    dot_general x4, matrix products, one_block(): jnp.einsum('rhk,rhe->khe', local_weight, grad_blk, preferred_element_type...  35.7 us
    dot_general x4, matrix products, one_block(): jnp.einsum('rhe,khe->rhk', grad_blk, cand_value, preferred_element_type=j...  29.3 us
    reduce_scatter x1, waiting for transfers between devices, on_device(): lax.psum_scatter(feature_terms, 'feat', scatter_dimension=1, tiled=True)  28.4 us
    convert_element_type x4, other arithmetic, one_block(): (local_prob * (local_dp - delta) * score_scale).astype(jnp.bfloat16)  28.3 us
    scatter-add x1, other arithmetic, on_device(): pair_grad.at[send_rows[0].reshape(-1)]  23.4 us
    scatter x4, local copies, waits for them, and re-layouts, on_device(): placed = jnp.zeros_like(joined).at[row_order].set(joined)  22 us
  transfers between devices with their start and end apart: 13, of which 6 were waited for; matrix products, arithmetic and copies ran while one was open for 21% of the time, Pallas kernels for 0%

commit v1 on v0

--- a/solution.py
+++ b/solution.py
@@ -61,7 +61,7 @@
     is_owner = global_ids // node_dev == my_index
     local_ids = global_ids % node_dev
     picked = jnp.where(is_owner[:, None], paired[local_ids].astype(jnp.float32), 0.0)
-    global_pairs = lax.psum(picked.astype(jnp.bfloat16), "dom")
+    global_pairs = jnp.sum(lax.all_gather(picked.astype(jnp.bfloat16), "dom"), axis=0)
     global_key = global_pairs[:, :col_count].reshape(-1, heads_here, HEAD)
     global_value = global_pairs[:, col_count:].reshape(-1, heads_here, HEAD)
     rows_blk = min(256, node_dev)

time: 594 us -> 530 us (0.89)
  waiting for transfers between devices: 186 us -> 115 us
    psum x1 -> x0, waiting for transfers between devices: 93.9 us -> none  [on_device(): global_pairs = lax.psum(picked.astype(jnp.bfloat16), 'dom')]
    ppermute x8, waiting for transfers between devices: 15.3 us -> 37.9 us  [swapped_2(): lax.ppermute(value, axis, [(i, i ^ 1 << bit) for i in range(lax.axis_size...]
  transfers between devices with their start and end apart: 13 -> 13, of which waited for: 6 -> 7; matrix products, arithmetic and copies ran while one was open for 21% -> 21% of each run, Pallas kernels for 0% -> 0%
where the time goes in v1:
time: 530 us; the launch traced here: 521 us
  matrix products  131 us (25%)
  local copies, waits for them, and re-layouts  116 us (22%)
  waiting for transfers between devices  115 us (22%)
  other arithmetic  109 us (21%)
  starting transfers between devices  28.3 us (5%)
  between operations  14.5 us (3%)
  loops' own time  7.21 us (1%)
    psum x1, waiting for transfers between devices, on_device(): lax.psum(global_grad.astype(jnp.bfloat16), 'dom').astype(jnp.float32)  48.2 us
    ppermute x8, waiting for transfers between devices, swapped_2(): lax.ppermute(value, axis, [(i, i ^ 1 << bit) for i in range(lax.axis_size...  37.9 us
    dot_general x4, matrix products, one_block(): jnp.einsum('rhk,rhe->khe', local_weight, grad_blk, preferred_element_type...  35.7 us
    dot_general x4, matrix products, one_block(): jnp.einsum('rhe,khe->rhk', grad_blk, cand_value, preferred_element_type=j...  29.3 us
    reduce_scatter x1, waiting for transfers between devices, on_device(): lax.psum_scatter(feature_terms, 'feat', scatter_dimension=1, tiled=True)  28.4 us
    convert_element_type x4, other arithmetic, one_block(): (local_prob * (local_dp - delta) * score_scale).astype(jnp.bfloat16)  28.3 us
    scatter-add x1, other arithmetic, on_device(): pair_grad.at[send_rows[0].reshape(-1)]  23.4 us
    scatter x4, local copies, waits for them, and re-layouts, on_device(): placed = jnp.zeros_like(joined).at[row_order].set(joined)  22 us
  transfers between devices with their start and end apart: 13, of which 7 were waited for; matrix products, arithmetic and copies ran while one was open for 21% of the time, Pallas kernels for 0%

profile of v1, /device:TPU:1, one launch (start us, length us, event | category | flops | bytes accessed | tf_op | source)
XLA Modules:
  0.0 521.2 jit_solution(17090711080600719638)
XLA Ops:
  11.2 16.9 %gather_fusion = bf16[4096,256]{1,0:T(8,128)(2,1)} fusion(bf16[1024,256]{1,0:T(8,128)(2,1)S(1)} %pad_maximum_fusion.8, s32[4096]{0:T(1024)S(1)} %fusion.60), kind=kCustom, calls=%fused_computation | custom fusion | bytes 4210688 | tf_op jit(solution)/shard_map/gather | solution.py:44
  28.1 9.6 %all-to-all-start = ((bf16[32,128,256]{2,1,0:T(8,128)(2,1)}), bf16[32,128,256]{2,1,0:T(8,128)(2,1)}, u32[]{:S(2)}, u32[]{:S(2)}) async-start(bf16[32,128,256]{2,1,0:T(8,128)(2,1)} %bitcast.337), calls=%async_computation | async-start | bytes 4194304 | tf_op jit(solution)/shard_map/all_to_all | solution.py:45
  41.4 2.7 collective-permute-start.2
  54.4 20.6 %collective-permute-done.3 = bf16[1024,256]{1,0:T(8,128)(2,1)} collective-permute-done((bf16[1024,256]{1,0:T(8,128)(2,1)S(1)}, bf16[1024,256]{1,0:T(8,128)(2,1)}, u32[]{:S(2)}, u32[]{:S(2)}) %collective-permute-start.3) | collective-permute-done | bytes 524320 | tf_op jit(solution)/shard_map/ppermute | solution.py:13
  75.0 5.1 gather_fusion.4
  80.1 3.9 gather_fusion.3
  86.0 4.9 gather_fusion.2
  91.0 4.9 gather_fusion.1
  97.4 3.0 fusion.65
  101.9 2.3 copy.170
  105.9 2.1 pad_maximum_fusion.2
  111.4 214.5 %while.25 = (s32[]{:T(128)}, f32[5120,2,64]{0,2,1:T(8,128)}, f32[5120,2,64]{0,2,1:T(8,128)}, f32[128,2,64]{0,2,1:T(8,128)}, f32[128,2,64]{0,2,1:T(8,128)}, /*ind...) while((s32[]{:T(128)}, f32[5120,2,64]{0,2,1:T(8,128)}, ...), condition=%wide.region_11.12_spmd.clone, body=%wide.region_1.11_spmd.clone.sunk | while | flops 2151969280 | bytes 260051440 | solution.py:168
  120.4 3.6 bitcast_reduce_fusion.2
  124.1 3.0 fusion.165
  128.1 4.2 fusion.174
  133.7 8.3 %fusion.170 = f32[5120,2,64]{0,2,1:T(8,128)} fusion(bf16[256,2,64]{0,2,1:T(8,128)(2,1)S(1)} %bitcast.353, f32[5120,2,64]{0,2,1:T(8,128)} %get-tuple-element.548, pred[]{:T(512)S(6)} %compare.7, f32[2,256,5120]{2,1,0:T(8,128)} %copy-done.2, f32[256,2]{0,1:T(2,128)S(1)} %add_add_fusion.5, f32[256,2]{0,1:T(2,128)S(1)} %maximum_maximum_fusion.2, ...), kind=kOutput, calls=%fused_computation.25.clone.1 | convolution fusion | flops 349962240 | bytes 17108992 | tf_op jit(solution)/shard_map/while/body/eval_jaxpr/rhk,rhe->khe/dot_general | solution.py:152
  142.0 7.3 %fusion.167 = (f32[256,2]{0,1:T(2,128)S(1)}, f32[2,256,5120]{2,1,0:T(8,128)}) fusion(f32[256,2]{0,1:T(2,128)S(1)} %add_add_fusion.5, f32[256,2]{0,1:T(2,128)S(1)} %maximum_maximum_fusion.2, f32[2,256,5120]{2,1,0:T(8,128)S(1)} %bitcast.327, pred[256,5120]{1,0:T(8,128)(4,1)S(1)} %bitcast_and_fusion.2, bf16[256,2,64]{0,2,1:T(8,128)(2,1)S(1)} %bitcast.354, ...), kind=kOutput, calls=%fused_computation.14.clone.1 | convolution fusion | flops 351272448 | bytes 23664640 | tf_op jit(solution)/shard_map/while/body/eval_jaxpr/rhe,khe->rhk/dot_general | solution.py:125
  149.5 7.1 %fusion.168 = bf16[256,2,5120]{2,0,1:T(8,128)(2,1)S(1)} fusion(f32[2,256,5120]{2,1,0:T(8,128)} %get-tuple-element.506, f32[256,2]{0,1:T(2,128)S(1)} %add_add_fusion.6, f32[256,2]{0,1:T(2,128)S(1)} %add_add_fusion.5, f32[256,2]{0,1:T(2,128)S(1)} %maximum_maximum_fusion.2, f32[2,256,5120]{2,1,0:T(8,128)S(1)} %bitcast.327, ...), kind=kLoop, calls=%fused_computation.17.clone.1 | loop fusion | flops 20971520 | bytes 27531264 | tf_op jit(solution)/shard_map/while/body/eval_jaxpr/convert_element_type | solution.py:139
  172.6 3.6 bitcast_reduce_fusion.2
  176.3 3.0 fusion.165
  180.3 4.2 fusion.174
  186.8 9.1 %fusion.170 = f32[5120,2,64]{0,2,1:T(8,128)} fusion(bf16[256,2,64]{0,2,1:T(8,128)(2,1)S(1)} %bitcast.353, f32[5120,2,64]{0,2,1:T(8,128)} %get-tuple-element.548, pred[]{:T(512)S(6)} %compare.7, f32[2,256,5120]{2,1,0:T(8,128)} %copy-done.2, f32[256,2]{0,1:T(2,128)S(1)} %add_add_fusion.5, f32[256,2]{0,1:T(2,128)S(1)} %maximum_maximum_fusion.2, ...), kind=kOutput, calls=%fused_computation.25.clone.1 | convolution fusion | flops 349962240 | bytes 17108992 | tf_op jit(solution)/shard_map/while/body/eval_jaxpr/rhk,rhe->khe/dot_general | solution.py:152
  195.9 7.3 %fusion.167 = (f32[256,2]{0,1:T(2,128)S(1)}, f32[2,256,5120]{2,1,0:T(8,128)}) fusion(f32[256,2]{0,1:T(2,128)S(1)} %add_add_fusion.5, f32[256,2]{0,1:T(2,128)S(1)} %maximum_maximum_fusion.2, f32[2,256,5120]{2,1,0:T(8,128)S(1)} %bitcast.327, pred[256,5120]{1,0:T(8,128)(4,1)S(1)} %bitcast_and_fusion.2, bf16[256,2,64]{0,2,1:T(8,128)(2,1)S(1)} %bitcast.354, ...), kind=kOutput, calls=%fused_computation.14.clone.1 | convolution fusion | flops 351272448 | bytes 23664640 | tf_op jit(solution)/shard_map/while/body/eval_jaxpr/rhe,khe->rhk/dot_general | solution.py:125
  203.4 7.1 %fusion.168 = bf16[256,2,5120]{2,0,1:T(8,128)(2,1)S(1)} fusion(f32[2,256,5120]{2,1,0:T(8,128)} %get-tuple-element.506, f32[256,2]{0,1:T(2,128)S(1)} %add_add_fusion.6, f32[256,2]{0,1:T(2,128)S(1)} %add_add_fusion.5, f32[256,2]{0,1:T(2,128)S(1)} %maximum_maximum_fusion.2, f32[2,256,5120]{2,1,0:T(8,128)S(1)} %bitcast.327, ...), kind=kLoop, calls=%fused_computation.17.clone.1 | loop fusion | flops 20971520 | bytes 27531264 | tf_op jit(solution)/shard_map/while/body/eval_jaxpr/convert_element_type | solution.py:139
  226.5 3.6 bitcast_reduce_fusion.2
  230.2 3.0 fusion.165
  234.3 4.2 fusion.174
  240.7 9.1 %fusion.170 = f32[5120,2,64]{0,2,1:T(8,128)} fusion(bf16[256,2,64]{0,2,1:T(8,128)(2,1)S(1)} %bitcast.353, f32[5120,2,64]{0,2,1:T(8,128)} %get-tuple-element.548, pred[]{:T(512)S(6)} %compare.7, f32[2,256,5120]{2,1,0:T(8,128)} %copy-done.2, f32[256,2]{0,1:T(2,128)S(1)} %add_add_fusion.5, f32[256,2]{0,1:T(2,128)S(1)} %maximum_maximum_fusion.2, ...), kind=kOutput, calls=%fused_computation.25.clone.1 | convolution fusion | flops 349962240 | bytes 17108992 | tf_op jit(solution)/shard_map/while/body/eval_jaxpr/rhk,rhe->khe/dot_general | solution.py:152
  249.9 7.3 %fusion.167 = (f32[256,2]{0,1:T(2,128)S(1)}, f32[2,256,5120]{2,1,0:T(8,128)}) fusion(f32[256,2]{0,1:T(2,128)S(1)} %add_add_fusion.5, f32[256,2]{0,1:T(2,128)S(1)} %maximum_maximum_fusion.2, f32[2,256,5120]{2,1,0:T(8,128)S(1)} %bitcast.327, pred[256,5120]{1,0:T(8,128)(4,1)S(1)} %bitcast_and_fusion.2, bf16[256,2,64]{0,2,1:T(8,128)(2,1)S(1)} %bitcast.354, ...), kind=kOutput, calls=%fused_computation.14.clone.1 | convolution fusion | flops 351272448 | bytes 23664640 | tf_op jit(solution)/shard_map/while/body/eval_jaxpr/rhe,khe->rhk/dot_general | solution.py:125
  257.3 7.1 %fusion.168 = bf16[256,2,5120]{2,0,1:T(8,128)(2,1)S(1)} fusion(f32[2,256,5120]{2,1,0:T(8,128)} %get-tuple-element.506, f32[256,2]{0,1:T(2,128)S(1)} %add_add_fusion.6, f32[256,2]{0,1:T(2,128)S(1)} %add_add_fusion.5, f32[256,2]{0,1:T(2,128)S(1)} %maximum_maximum_fusion.2, f32[2,256,5120]{2,1,0:T(8,128)S(1)} %bitcast.327, ...), kind=kLoop, calls=%fused_computation.17.clone.1 | loop fusion | flops 20971520 | bytes 27531264 | tf_op jit(solution)/shard_map/while/body/eval_jaxpr/convert_element_type | solution.py:139
  280.5 3.6 bitcast_reduce_fusion.2
  284.1 3.0 fusion.165
  288.1 4.2 fusion.174
  294.6 9.1 %fusion.170 = f32[5120,2,64]{0,2,1:T(8,128)} fusion(bf16[256,2,64]{0,2,1:T(8,128)(2,1)S(1)} %bitcast.353, f32[5120,2,64]{0,2,1:T(8,128)} %get-tuple-element.548, pred[]{:T(512)S(6)} %compare.7, f32[2,256,5120]{2,1,0:T(8,128)} %copy-done.2, f32[256,2]{0,1:T(2,128)S(1)} %add_add_fusion.5, f32[256,2]{0,1:T(2,128)S(1)} %maximum_maximum_fusion.2, ...), kind=kOutput, calls=%fused_computation.25.clone.1 | convolution fusion | flops 349962240 | bytes 17108992 | tf_op jit(solution)/shard_map/while/body/eval_jaxpr/rhk,rhe->khe/dot_general | solution.py:152
  303.7 7.3 %fusion.167 = (f32[256,2]{0,1:T(2,128)S(1)}, f32[2,256,5120]{2,1,0:T(8,128)}) fusion(f32[256,2]{0,1:T(2,128)S(1)} %add_add_fusion.5, f32[256,2]{0,1:T(2,128)S(1)} %maximum_maximum_fusion.2, f32[2,256,5120]{2,1,0:T(8,128)S(1)} %bitcast.327, pred[256,5120]{1,0:T(8,128)(4,1)S(1)} %bitcast_and_fusion.2, bf16[256,2,64]{0,2,1:T(8,128)(2,1)S(1)} %bitcast.354, ...), kind=kOutput, calls=%fused_computation.14.clone.1 | convolution fusion | flops 351272448 | bytes 23664640 | tf_op jit(solution)/shard_map/while/body/eval_jaxpr/rhe,khe->rhk/dot_general | solution.py:125
  311.2 7.1 %fusion.168 = bf16[256,2,5120]{2,0,1:T(8,128)(2,1)S(1)} fusion(f32[2,256,5120]{2,1,0:T(8,128)} %get-tuple-element.506, f32[256,2]{0,1:T(2,128)S(1)} %add_add_fusion.6, f32[256,2]{0,1:T(2,128)S(1)} %add_add_fusion.5, f32[256,2]{0,1:T(2,128)S(1)} %maximum_maximum_fusion.2, f32[2,256,5120]{2,1,0:T(8,128)S(1)} %bitcast.327, ...), kind=kLoop, calls=%fused_computation.17.clone.1 | loop fusion | flops 20971520 | bytes 27531264 | tf_op jit(solution)/shard_map/while/body/eval_jaxpr/convert_element_type | solution.py:139
  333.6 7.3 %all-to-all-start.1 = ((bf16[32,128,256]{1,2,0:T(8,128)(2,1)}), bf16[32,128,256]{1,2,0:T(8,128)(2,1)}, u32[]{:S(2)}, u32[]{:S(2)}) async-start(bf16[32,128,256]{1,2,0:T(8,128)(2,1)} %copy.119), calls=%async_computation.1 | async-start | bytes 4194304 | tf_op jit(solution)/shard_map/all_to_all | solution.py:183
  344.9 5.5 %scatter_custom_fusion = f32[1024,256]{1,0:T(8,128)S(1)} fusion(s32[1024]{0:T(1024)} %bitcast.373, f32[1024,256]{1,0:T(8,128)} %copy.115, f32[]{:T(128)} %constant.41.clone.1), kind=kCustom, calls=%fused_computation.117 | custom fusion | bytes 1049088 | tf_op jit(solution)/shard_map/scatter | solution.py:201
  353.8 5.5 %scatter_custom_fusion.1 = f32[1024,256]{1,0:T(8,128)S(1)} fusion(s32[1024]{0:T(1024)} %bitcast.371, f32[1024,256]{1,0:T(8,128)} %copy.116, f32[]{:T(128)} %constant.41.clone.1), kind=kCustom, calls=%fused_computation.115 | custom fusion | bytes 1049088 | tf_op jit(solution)/shard_map/scatter | solution.py:201
  361.6 5.5 %scatter_custom_fusion.2 = f32[1024,256]{1,0:T(8,128)S(1)} fusion(s32[1024]{0:T(1024)} %bitcast.369, f32[1024,256]{1,0:T(8,128)} %copy.117, f32[]{:T(128)} %constant.41.clone.1), kind=kCustom, calls=%fused_computation.113 | custom fusion | bytes 1049088 | tf_op jit(solution)/shard_map/scatter | solution.py:201
  368.4 5.4 %scatter_custom_fusion.3 = f32[1024,256]{1,0:T(8,128)S(1)} fusion(s32[1024]{0:T(1024)} %bitcast.367, f32[1024,256]{1,0:T(8,128)S(1)} %copy.118, f32[]{:T(128)} %constant.41.clone.1), kind=kCustom, calls=%fused_computation.111 | custom fusion | bytes 1049088 | tf_op jit(solution)/shard_map/scatter | solution.py:201
  376.1 2.7 collective-permute-start.6
  388.3 2.5 collective-permute-done.6
  390.8 11.4 %collective-permute-done.5 = bf16[1024,256]{1,0:T(8,128)(2,1)} collective-permute-done((bf16[1024,256]{1,0:T(8,128)(2,1)}, bf16[1024,256]{1,0:T(8,128)(2,1)}, u32[]{:S(2)}, u32[]{:S(2)}) %collective-permute-start.5) | collective-permute-done | bytes 524320 | tf_op jit(solution)/shard_map/ppermute | solution.py:13
  404.0 4.1 copy.120
  408.1 23.4 %scatter_custom_fusion.4 = f32[1024,256]{1,0:T(8,128)S(1)} fusion(f32[1024,256]{1,0:T(8,128)S(1)} %fusion.41, s32[4096]{0:T(1024)S(1)} %bitcast.365, bf16[4096,256]{1,0:T(8,128)(2,1)} %bitcast.336), kind=kCustom, calls=%fused_computation.82 | custom fusion | flops 2097152 | bytes 3145728 | tf_op jit(solution)/shard_map/scatter-add | solution.py:186
  431.5 48.2 %all-reduce.3.cloned.1.call-done = bf16[128,256]{1,0:T(8,128)(2,1)} async-done(((bf16[128,256]{1,0:T(8,128)(2,1)}), bf16[128,256]{1,0:T(8,128)(2,1)}) %all-reduce.3.cloned.1.call-update) | async-done | bytes 65552 | tf_op jit(solution)/shard_map/psum | solution.py:208
  484.2 28.4 %reduce-scatter.2.cloned.1.call-done = f32[1024,128]{1,0:T(8,128)} async-done(((f32[1024,512]{1,0:T(8,128)}), f32[1024,128]{1,0:T(8,128)}) %reduce-scatter.2.cloned.1.call-update) | async-done | bytes 524304 | tf_op jit(solution)/shard_map/reduce_scatter | solution.py:223
  (439 shorter events, 137.0 us)
Async XLA Ops:
  11.1 17.0 %copy-start.14 = (bf16[1024,128]{1,0:T(8,128)(2,1)}, bf16[1024,128]{1,0:T(8,128)(2,1)S(1)}, u32[]{:S(2)}) copy-start(bf16[1024,128]{1,0:T(8,128)(2,1)S(1)} %convolution_convert_fusion) | copy-start | bytes 786436
  28.1 9.7 %copy-start.36 = (s32[128]{0:T(128)S(1)}, s32[128]{0:T(128)}, u32[]{:S(2)}) copy-start(s32[128]{0:T(128)} %param.21) | copy-start | bytes 1540
  28.1 17.5 %copy-start.28 = (s32[4,1024]{1,0:T(4,128)S(1)}, s32[4,1024]{1,0:T(4,128)}, u32[]{:S(2)}) copy-start(s32[4,1024]{1,0:T(4,128)} %param.20) | copy-start | bytes 49156
  28.1 25.1 %copy-start.21 = (bf16[512,128]{1,0:T(8,128)(2,1)S(1)}, bf16[512,128]{1,0:T(8,128)(2,1)}, u32[]{:S(2)}) copy-start(bf16[512,128]{1,0:T(8,128)(2,1)} %param.13) | copy-start | bytes 393220
  28.1 69.3 %all-to-all-start = ((bf16[32,128,256]{2,1,0:T(8,128)(2,1)}), bf16[32,128,256]{2,1,0:T(8,128)(2,1)}, u32[]{:S(2)}, u32[]{:S(2)}) async-start(bf16[32,128,256]{2,1,0:T(8,128)(2,1)} %bitcast.337), calls=%async_computation | async-start | bytes 4194304 | tf_op jit(solution)/shard_map/all_to_all | solution.py:45
  37.7 70.3 %all-gather.2.cloned.1.call-start = ((), (), s32[]{:S(2)}) async-start(), calls=%async_computation.3 | async-start | bytes 2162688 | tf_op jit(solution)/shard_map/all_gather | solution.py:64
  39.9 35.1 %collective-permute-start.3 = (bf16[1024,256]{1,0:T(8,128)(2,1)S(1)}, bf16[1024,256]{1,0:T(8,128)(2,1)}, u32[]{:S(2)}, u32[]{:S(2)}) collective-permute-start(bf16[1024,256]{1,0:T(8,128)(2,1)S(1)} %pad_maximum_fusion.8), channel_id=1, source_target_pairs={{0,32},{4,36},{8,40},{12,44},{16,48},{20,52},{24,56},{28,60},{32,0... | collective-permute-start | bytes 1572872 | tf_op jit(solution)/shard_map/ppermute | solution.py:13
  41.4 38.7 %collective-permute-start.2 = (bf16[1024,256]{1,0:T(8,128)(2,1)S(1)}, bf16[1024,256]{1,0:T(8,128)(2,1)S(1)}, u32[]{:S(2)}, u32[]{:S(2)}) collective-permute-start(bf16[1024,256]{1,0:T(8,128)(2,1)S(1)} %pad_maximum_fusion.8), channel_id=1, source_target_pairs={{0,16},{4,20},{8,24},{12,28},{16,0},{20,4},{24,8},{28,12},{32,48},... | collective-permute-start | bytes 1572872 | tf_op jit(solution)/shard_map/ppermute | solution.py:13
  44.1 42.0 %collective-permute-start.1 = (bf16[1024,256]{1,0:T(8,128)(2,1)S(1)}, bf16[1024,256]{1,0:T(8,128)(2,1)S(1)}, u32[]{:S(2)}, u32[]{:S(2)}) collective-permute-start(bf16[1024,256]{1,0:T(8,128)(2,1)S(1)} %pad_maximum_fusion.8), channel_id=1, source_target_pairs={{0,8},{4,12},{8,0},{12,4},{16,24},{20,28},{24,16},{28,20},{32,40},... | collective-permute-start | bytes 1572872 | tf_op jit(solution)/shard_map/ppermute | solution.py:13
  44.4 46.6 %collective-permute-start = (bf16[1024,256]{1,0:T(8,128)(2,1)S(1)}, bf16[1024,256]{1,0:T(8,128)(2,1)S(1)}, u32[]{:S(2)}, u32[]{:S(2)}) collective-permute-start(bf16[1024,256]{1,0:T(8,128)(2,1)S(1)} %pad_maximum_fusion.8), channel_id=1, source_target_pairs={{0,4},{4,0},{8,12},{12,8},{16,20},{20,16},{24,28},{28,24},{32,36},... | collective-permute-start | bytes 1572872 | tf_op jit(solution)/shard_map/ppermute | solution.py:13
  133.4 8.6 %slice-start = ((s8[10485760]{0:T(1024)(128)(4,1)}), s8[4194304]{0:T(1024)(128)(4,1)S(1)}, s32[]{:S(2)}) async-start(s8[10485760]{0:T(1024)(128)(4,1)} %bitcast.326), calls=%async_computation.6 | async-start | bytes 8388608 | tf_op jit(solution)/shard_map/while
  133.7 8.4 %slice-start.1 = ((s8[10485760]{0:T(1024)(128)(4,1)}), s8[4194304]{0:T(1024)(128)(4,1)S(1)}, s32[]{:S(2)}) async-start(s8[10485760]{0:T(1024)(128)(4,1)} %bitcast.326), calls=%async_computation.7 | async-start | bytes 8388608 | tf_op jit(solution)/shard_map/while
  133.7 8.4 %slice-start.2 = ((s8[10485760]{0:T(1024)(128)(4,1)}), s8[2097152]{0:T(1024)(128)(4,1)S(1)}, s32[]{:S(2)}) async-start(s8[10485760]{0:T(1024)(128)(4,1)} %bitcast.326), calls=%async_computation.8 | async-start | bytes 4194304 | tf_op jit(solution)/shard_map/while
  133.7 8.3 %copy-start.19 = (bf16[5120,2,64]{0,2,1:T(8,128)(2,1)S(1)}, bf16[5120,2,64]{0,2,1:T(8,128)(2,1)}, u32[]{:S(2)}) copy-start(bf16[5120,2,64]{0,2,1:T(8,128)(2,1)} %get-tuple-element.589) | copy-start | bytes 3932164 | tf_op jit(solution)/shard_map/while
  149.5 8.9 %copy-start.5 = (bf16[5120,2,64]{0,2,1:T(8,128)(2,1)S(1)}, bf16[5120,2,64]{0,2,1:T(8,128)(2,1)}, u32[]{:S(2)}) copy-start(bf16[5120,2,64]{0,2,1:T(8,128)(2,1)} %get-tuple-element.585) | copy-start | bytes 3932164 | tf_op jit(solution)/shard_map/while
  186.5 9.4 %slice-start = ((s8[10485760]{0:T(1024)(128)(4,1)}), s8[4194304]{0:T(1024)(128)(4,1)S(1)}, s32[]{:S(2)}) async-start(s8[10485760]{0:T(1024)(128)(4,1)} %bitcast.326), calls=%async_computation.6 | async-start | bytes 8388608 | tf_op jit(solution)/shard_map/while
  186.7 9.2 %slice-start.1 = ((s8[10485760]{0:T(1024)(128)(4,1)}), s8[4194304]{0:T(1024)(128)(4,1)S(1)}, s32[]{:S(2)}) async-start(s8[10485760]{0:T(1024)(128)(4,1)} %bitcast.326), calls=%async_computation.7 | async-start | bytes 8388608 | tf_op jit(solution)/shard_map/while
  186.7 9.2 %slice-start.2 = ((s8[10485760]{0:T(1024)(128)(4,1)}), s8[2097152]{0:T(1024)(128)(4,1)S(1)}, s32[]{:S(2)}) async-start(s8[10485760]{0:T(1024)(128)(4,1)} %bitcast.326), calls=%async_computation.8 | async-start | bytes 4194304 | tf_op jit(solution)/shard_map/while
  186.8 9.2 %copy-start.19 = (bf16[5120,2,64]{0,2,1:T(8,128)(2,1)S(1)}, bf16[5120,2,64]{0,2,1:T(8,128)(2,1)}, u32[]{:S(2)}) copy-start(bf16[5120,2,64]{0,2,1:T(8,128)(2,1)} %get-tuple-element.589) | copy-start | bytes 3932164 | tf_op jit(solution)/shard_map/while
  203.3 7.8 %copy-start.11 = (f32[128,2,64]{0,2,1:T(8,128)S(1)}, f32[128,2,64]{0,2,1:T(8,128)}, u32[]{:S(2)}) copy-start(f32[128,2,64]{0,2,1:T(8,128)} %get-tuple-element.549) | copy-start | bytes 196612 | tf_op jit(solution)/shard_map/while
  203.3 8.9 %copy-start.5 = (bf16[5120,2,64]{0,2,1:T(8,128)(2,1)S(1)}, bf16[5120,2,64]{0,2,1:T(8,128)(2,1)}, u32[]{:S(2)}) copy-start(bf16[5120,2,64]{0,2,1:T(8,128)(2,1)} %get-tuple-element.585) | copy-start | bytes 3932164 | tf_op jit(solution)/shard_map/while
  240.5 9.4 %slice-start = ((s8[10485760]{0:T(1024)(128)(4,1)}), s8[4194304]{0:T(1024)(128)(4,1)S(1)}, s32[]{:S(2)}) async-start(s8[10485760]{0:T(1024)(128)(4,1)} %bitcast.326), calls=%async_computation.6 | async-start | bytes 8388608 | tf_op jit(solution)/shard_map/while
  240.7 9.2 %slice-start.1 = ((s8[10485760]{0:T(1024)(128)(4,1)}), s8[4194304]{0:T(1024)(128)(4,1)S(1)}, s32[]{:S(2)}) async-start(s8[10485760]{0:T(1024)(128)(4,1)} %bitcast.326), calls=%async_computation.7 | async-start | bytes 8388608 | tf_op jit(solution)/shard_map/while
  240.7 9.2 %slice-start.2 = ((s8[10485760]{0:T(1024)(128)(4,1)}), s8[2097152]{0:T(1024)(128)(4,1)S(1)}, s32[]{:S(2)}) async-start(s8[10485760]{0:T(1024)(128)(4,1)} %bitcast.326), calls=%async_computation.8 | async-start | bytes 4194304 | tf_op jit(solution)/shard_map/while
  240.7 9.2 %copy-start.19 = (bf16[5120,2,64]{0,2,1:T(8,128)(2,1)S(1)}, bf16[5120,2,64]{0,2,1:T(8,128)(2,1)}, u32[]{:S(2)}) copy-start(bf16[5120,2,64]{0,2,1:T(8,128)(2,1)} %get-tuple-element.589) | copy-start | bytes 3932164 | tf_op jit(solution)/shard_map/while
  257.3 8.9 %copy-start.5 = (bf16[5120,2,64]{0,2,1:T(8,128)(2,1)S(1)}, bf16[5120,2,64]{0,2,1:T(8,128)(2,1)}, u32[]{:S(2)}) copy-start(bf16[5120,2,64]{0,2,1:T(8,128)(2,1)} %get-tuple-element.585) | copy-start | bytes 3932164 | tf_op jit(solution)/shard_map/while
  294.3 9.4 %slice-start = ((s8[10485760]{0:T(1024)(128)(4,1)}), s8[4194304]{0:T(1024)(128)(4,1)S(1)}, s32[]{:S(2)}) async-start(s8[10485760]{0:T(1024)(128)(4,1)} %bitcast.326), calls=%async_computation.6 | async-start | bytes 8388608 | tf_op jit(solution)/shard_map/while
  294.5 9.2 %slice-start.1 = ((s8[10485760]{0:T(1024)(128)(4,1)}), s8[4194304]{0:T(1024)(128)(4,1)S(1)}, s32[]{:S(2)}) async-start(s8[10485760]{0:T(1024)(128)(4,1)} %bitcast.326), calls=%async_computation.7 | async-start | bytes 8388608 | tf_op jit(solution)/shard_map/while
  294.5 9.2 %slice-start.2 = ((s8[10485760]{0:T(1024)(128)(4,1)}), s8[2097152]{0:T(1024)(128)(4,1)S(1)}, s32[]{:S(2)}) async-start(s8[10485760]{0:T(1024)(128)(4,1)} %bitcast.326), calls=%async_computation.8 | async-start | bytes 4194304 | tf_op jit(solution)/shard_map/while
  294.6 9.2 %copy-start.19 = (bf16[5120,2,64]{0,2,1:T(8,128)(2,1)S(1)}, bf16[5120,2,64]{0,2,1:T(8,128)(2,1)}, u32[]{:S(2)}) copy-start(bf16[5120,2,64]{0,2,1:T(8,128)(2,1)} %get-tuple-element.589) | copy-start | bytes 3932164 | tf_op jit(solution)/shard_map/while
  311.1 8.9 %copy-start.5 = (bf16[5120,2,64]{0,2,1:T(8,128)(2,1)S(1)}, bf16[5120,2,64]{0,2,1:T(8,128)(2,1)}, u32[]{:S(2)}) copy-start(bf16[5120,2,64]{0,2,1:T(8,128)(2,1)} %get-tuple-element.585) | copy-start | bytes 3932164 | tf_op jit(solution)/shard_map/while
  333.6 70.4 %all-to-all-start.1 = ((bf16[32,128,256]{1,2,0:T(8,128)(2,1)}), bf16[32,128,256]{1,2,0:T(8,128)(2,1)}, u32[]{:S(2)}, u32[]{:S(2)}) async-start(bf16[32,128,256]{1,2,0:T(8,128)(2,1)} %copy.119), calls=%async_computation.1 | async-start | bytes 4194304 | tf_op jit(solution)/shard_map/all_to_all | solution.py:183
  340.9 138.8 %all-reduce.3.cloned.1.call-start = ((), (), s32[]{:S(2)}) async-start(), calls=%async_computation.4 | async-start | bytes 131072 | tf_op jit(solution)/shard_map/psum | solution.py:208
  368.1 12.2 %copy-start.26 = (s32[1,32,128]{2,1,0:T(8,128)S(1)}, s32[1,32,128]{2,1,0:T(8,128)}, u32[]{:S(2)}) copy-start(s32[1,32,128]{2,1,0:T(8,128)} %param.17) | copy-start | bytes 49156
  368.4 14.1 %copy-start.13 = (f32[128,2,64]{0,2,1:T(8,128)S(1)}, f32[128,2,64]{0,2,1:T(8,128)}, u32[]{:S(2)}) copy-start(f32[128,2,64]{0,2,1:T(8,128)} %get-tuple-element.615) | copy-start | bytes 196612
  374.7 11.7 %copy-start.22 = (bf16[512,128]{1,0:T(8,128)(2,1)S(1)}, bf16[512,128]{1,0:T(8,128)(2,1)}, u32[]{:S(2)}) copy-start(bf16[512,128]{1,0:T(8,128)(2,1)} %param.13) | copy-start | bytes 393220
  374.7 11.7 %copy-start.25 = (bf16[4,256,128]{2,1,0:T(8,128)(2,1)S(1)}, bf16[4,256,128]{2,1,0:T(8,128)(2,1)}, u32[]{:S(2)}) copy-start(bf16[4,256,128]{2,1,0:T(8,128)(2,1)} %get-tuple-element.618) | copy-start | bytes 786436
  374.7 13.5 %collective-permute-start.7 = (bf16[1024,256]{1,0:T(8,128)(2,1)}, bf16[1024,256]{1,0:T(8,128)(2,1)}, u32[]{:S(2)}, u32[]{:S(2)}) collective-permute-start(bf16[1024,256]{1,0:T(8,128)(2,1)} %convert_element_type.145), channel_id=1, source_target_pairs={{0,32},{4,36},{8,40},{12,44},{16,48},{20,52},{24,56},{28,60},{32,0... | collective-permute-start | bytes 1572872 | tf_op jit(solution)/shard_map/ppermute | solution.py:13
  376.1 14.7 %collective-permute-start.6 = (bf16[1024,256]{1,0:T(8,128)(2,1)}, bf16[1024,256]{1,0:T(8,128)(2,1)}, u32[]{:S(2)}, u32[]{:S(2)}) collective-permute-start(bf16[1024,256]{1,0:T(8,128)(2,1)} %convert_element_type.143), channel_id=1, source_target_pairs={{0,16},{4,20},{8,24},{12,28},{16,0},{20,4},{24,8},{28,12},{32,48},... | collective-permute-start | bytes 1572872 | tf_op jit(solution)/shard_map/ppermute | solution.py:13
  378.8 23.3 %collective-permute-start.5 = (bf16[1024,256]{1,0:T(8,128)(2,1)}, bf16[1024,256]{1,0:T(8,128)(2,1)}, u32[]{:S(2)}, u32[]{:S(2)}) collective-permute-start(bf16[1024,256]{1,0:T(8,128)(2,1)} %convert_element_type.141), channel_id=1, source_target_pairs={{0,8},{4,12},{8,0},{12,4},{16,24},{20,28},{24,16},{28,20},{32,40},... | collective-permute-start | bytes 1572872 | tf_op jit(solution)/shard_map/ppermute | solution.py:13
  379.1 23.0 %collective-permute-start.4 = (bf16[1024,256]{1,0:T(8,128)(2,1)}, bf16[1024,256]{1,0:T(8,128)(2,1)}, u32[]{:S(2)}, u32[]{:S(2)}) collective-permute-start(bf16[1024,256]{1,0:T(8,128)(2,1)} %convert_element_type.139), channel_id=1, source_target_pairs={{0,4},{4,0},{8,12},{12,8},{16,20},{20,16},{24,28},{28,24},{32,36},... | collective-permute-start | bytes 1572872 | tf_op jit(solution)/shard_map/ppermute | solution.py:13
  384.3 128.4 %reduce-scatter.2.cloned.1.call-start = ((), (), s32[]{:S(2)}) async-start(), calls=%async_computation.5 | async-start | bytes 2621440 | tf_op jit(solution)/shard_map/reduce_scatter | solution.py:223
  386.4 15.7 %copy-start.16 = (f32[1024,128]{1,0:T(8,128)S(1)}, f32[1024,128]{1,0:T(8,128)}, u32[]{:S(2)}) copy-start(f32[1024,128]{1,0:T(8,128)} %copy.110) | copy-start | bytes 1572868
  386.4 15.7 %copy-start.17 = (f32[1024,128]{1,0:T(8,128)S(1)}, f32[1024,128]{1,0:T(8,128)}, u32[]{:S(2)}) copy-start(f32[1024,128]{1,0:T(8,128)} %copy.111) | copy-start | bytes 1572868
  408.1 71.7 %copy-start.34 = (pred[128]{0:T(512)(128)(4,1)S(1)}, pred[128]{0:T(512)(128)(4,1)}, u32[]{:S(2)}) copy-start(pred[128]{0:T(512)(128)(4,1)} %copy-done.33) | copy-start | bytes 388
  408.1 73.8 %copy-start.23 = (bf16[512,128]{1,0:T(8,128)(2,1)S(1)}, bf16[512,128]{1,0:T(8,128)(2,1)}, u32[]{:S(2)}) copy-start(bf16[512,128]{1,0:T(8,128)(2,1)} %param.14) | copy-start | bytes 393220
  431.5 50.8 %copy-start.24 = (bf16[512,128]{1,0:T(8,128)(2,1)S(1)}, bf16[512,128]{1,0:T(8,128)(2,1)}, u32[]{:S(2)}) copy-start(bf16[512,128]{1,0:T(8,128)(2,1)} %param.15) | copy-start | bytes 393220
  482.3 32.1 %copy-start.1 = (bf16[1024,512]{1,0:T(8,128)(2,1)S(1)}, bf16[1024,512]{1,0:T(8,128)(2,1)}, u32[]{:S(2)}) copy-start(bf16[1024,512]{1,0:T(8,128)(2,1)} %param.12) | copy-start | bytes 3145732
  (58 other events, 219.6 us)
Sparse Core Ops, SparseCore 0:
  40.8 57.7 all-gather.1
  384.4 95.2 all-reduce.2
  484.3 28.2 reduce-scatter.1
